TPU v7x, 32 devices: a whole 2x2x4 slice. The times are simulated.
32 devices in a mesh: ctx: 8 (over y, x, core), fsdp: 4 (over z).
Axes of the slice: x: 2, y: 2, z: 4, core: 2. Of those that a mesh axis runs over, the one named last changes fastest.
Arguments:
- hidden_in: bfloat16 [4, 1024, 2048], P('fsdp', 'ctx'), may hold values from -18 to 18
- out_grad: bfloat16 [4, 1024, 2048], P('fsdp', 'ctx'), may hold values from -6 to 6
- positions: int32 [4, 1024], P('fsdp', 'ctx'), may hold values from 0 to 1023, as said below
- block_order: int32 [16], replicated, may hold values from 0 to 15, as said below
- attn_gain: float32 [2048], replicated, may hold values from 0.25 to 1.75
- ffn_gain: float32 [2048], replicated, may hold values from 0.25 to 1.75
- qkv_weight: bfloat16 [2048, 3072], P('fsdp'), may hold values from -1 to 1
- out_weight: bfloat16 [2048, 2048], P('fsdp'), may hold values from -0.5 to 0.5
- ffn_weight: bfloat16 [2048, 3, 8192], P(None, None, 'fsdp'), may hold values from -0.125 to 0.125
Outputs:
- hidden_out: bfloat16 [4, 1024, 2048], P('fsdp', 'ctx')
- input_grad: float32 [4, 1024, 2048], P('fsdp', 'ctx')
- qkv_weight_grad: float32 [2048, 3072], P(('ctx', 'fsdp'))
- out_weight_grad: float32 [2048, 2048], P(('ctx', 'fsdp'))
- ffn_weight_grad: float32 [2048, 3, 8192], P('ctx', None, 'fsdp')
- attn_gain_grad: float32 [2048], P(('ctx', 'fsdp'))
- ffn_gain_grad: float32 [2048], P(('ctx', 'fsdp'))
Inputs may be any that keep to these rules, and one draw needn't show every extreme that they name: `block_order`: the two slots 2c and 2c + 1 hold two blocks whose numbers add up to 15, and every block number appears once. In initial token order, a sequence's positions rise by one from token to token and restart at 0 at its first token and at the start of each packed document; the first sequence is a single document; they are listed in storage order.
All inputs are finite; a program needn't handle non-finite values.
Results may differ from a plain program's by a relative error of at most 0.03.
Values may be sent and summed in bfloat16 or wider, within the bound.
No kernel may reach another device: no remote copies, remote signals or barrier semaphores. Data moves between devices by JAX's collectives and lax.ppermute only.
A program may use at most 576 MiB of HBM per device.

v0:
```python
import math
import jax
import jax.numpy as jnp
from jax import lax
from jax.sharding import PartitionSpec as P

H = 32
KV = 8
HD = 64
NORM_EPS = 1e-05
ROPE_BASE = 500000.0
block_rows = 512


def rotate(values, token_places):
    head_dim = values.shape[-1]
    half_dim = head_dim // 2
    frequency = jnp.power(ROPE_BASE, -(jnp.arange(half_dim, dtype=jnp.float32) * 2.0 / head_dim))
    angles = token_places.astype(jnp.float32)[:, None] * frequency[None, :]
    cosine = jnp.concatenate([jnp.cos(angles), jnp.cos(angles)], axis=-1)[:, None, :]
    sine_part = jnp.concatenate([jnp.sin(angles), jnp.sin(angles)], axis=-1)[:, None, :]
    turned = jnp.concatenate([-values[..., half_dim:], values[..., :half_dim]], axis=-1)
    return values * cosine + turned * sine_part


def norm_scale(values):
    return lax.rsqrt(jnp.mean(values * values, axis=-1, keepdims=True) + NORM_EPS)


def lookup(entries, row_ids):
    matches = row_ids[:, None] == jnp.arange(entries.shape[0], dtype=jnp.int32)[None, :]
    return jnp.sum(jnp.where(matches, entries[None, :], 0), axis=1)


def anchor_rows(block_order, first_row, row_count, block_len):
    row_ids = first_row + jnp.arange(row_count, dtype=jnp.int32)
    return lookup(block_order, row_ids // block_len) * block_len + row_ids % block_len


def sweep_keys(step_fn, carried, pieces):
    row_count = pieces[0].shape[0]
    full_blocks = row_count // block_rows

    def loop_step(step_index, carry_state):
        key_pair = tuple(
            (
                lax.dynamic_slice_in_dim(piece_rows, step_index * block_rows, block_rows, 0)
                for piece_rows in pieces
            )
        )
        return step_fn(carry_state, key_pair, step_index * block_rows)

    carried = lax.fori_loop(0, full_blocks, loop_step, carried)
    return carried


def body(
    hidden_in,
    out_grad,
    positions,
    block_order,
    attn_gain,
    ffn_gain,
    qkv_weight,
    out_weight,
    ffn_weight,
):
    local_rows = hidden_in.shape[1]
    block_len = local_rows // 2
    ctx_count = lax.axis_size("ctx")
    seq_rows = local_rows * ctx_count
    groups = H // KV
    score_scale = 1.0 / math.sqrt(HD)
    slot_first = 2 * lax.axis_index("ctx") * block_len
    own_anchor = anchor_rows(block_order, slot_first, local_rows, block_len)
    inputs = hidden_in[0].astype(jnp.float32)
    grad_in = out_grad[0]
    token_places = positions[0]
    scale_one = norm_scale(inputs)
    normed_one = (inputs * scale_one * attn_gain).astype(jnp.bfloat16)
    qkv_full, out_full = (
        lax.all_gather(qkv_weight, "fsdp", axis=0, tiled=True),
        lax.all_gather(out_weight, "fsdp", axis=0, tiled=True),
    )
    projected = jnp.dot(normed_one, qkv_full, preferred_element_type=jnp.float32)
    queries = rotate(projected[:, : H * HD].reshape(local_rows, H, HD), token_places).astype(
        jnp.bfloat16
    )
    queries = queries.reshape(local_rows, KV, groups, HD)
    key_local = rotate(
        projected[:, H * HD : (H + KV) * HD].reshape(local_rows, KV, HD), token_places
    ).astype(jnp.bfloat16)
    key_local = key_local.reshape(local_rows, KV * HD)
    value_local = projected[:, (H + KV) * HD :].astype(jnp.bfloat16)

    def masked_scores(key_heads, first_row, row_count):
        scores = (
            jnp.einsum("tkgd,skd->kgts", queries, key_heads, preferred_element_type=jnp.float32)
            * score_scale
        )
        allowed = (
            anchor_rows(block_order, first_row, row_count, block_len)[None, :]
            <= own_anchor[:, None]
        )[None, None]
        return (jnp.where(allowed, scores, -1e30), allowed)

    def forward_step(carry_state, key_pair, first_row):
        top_old, total_old, summed = carry_state
        key_part, value_part = key_pair
        row_count = key_part.shape[0]
        key_heads = key_part.reshape(row_count, KV, HD)
        value_heads = value_part.reshape(row_count, KV, HD)
        scores, allowed = masked_scores(key_heads, first_row, row_count)
        top_new = jnp.maximum(top_old, jnp.max(scores, axis=-1))
        weights = jnp.where(allowed, jnp.exp(scores - top_new[..., None]), 0.0)
        rescale = jnp.exp(top_old - top_new)
        total_new = total_old * rescale + jnp.sum(weights, axis=-1)
        summed = summed * rescale[..., None] + jnp.einsum(
            "kgts,skd->kgtd",
            weights.astype(jnp.bfloat16),
            value_heads,
            preferred_element_type=jnp.float32,
        )
        return (top_new, total_new, summed)

    start_state = (
        jnp.full((KV, groups, local_rows), -1e30, jnp.float32),
        jnp.zeros((KV, groups, local_rows), jnp.float32),
        jnp.zeros((KV, groups, local_rows, HD), jnp.float32),
    )
    attn_state = sweep_keys(
        forward_step,
        start_state,
        (
            lax.all_gather(key_local, "ctx", axis=0, tiled=True),
            lax.all_gather(value_local, "ctx", axis=0, tiled=True),
        ),
    )
    row_top, row_total, summed = attn_state
    log_total = row_top + jnp.log(row_total)
    attended = (summed / row_total[..., None]).transpose(2, 0, 1, 3)
    attn_rows = attended.reshape(local_rows, H * HD).astype(jnp.bfloat16)
    residual = inputs + jnp.einsum(
        "tc,dc->td", attn_rows, out_full, preferred_element_type=jnp.float32
    )
    scale_two = norm_scale(residual)
    normed_two = (residual * scale_two * ffn_gain).astype(jnp.bfloat16)
    rows_in, rows_out = (
        lax.all_gather(normed_two, "fsdp", axis=0, tiled=True),
        lax.all_gather(grad_in, "fsdp", axis=0, tiled=True),
    )
    weight_piece = lax.all_gather(ffn_weight, "fsdp", axis=2, tiled=True)
    gate_part = jnp.dot(normed_two, weight_piece[:, 0, :], preferred_element_type=jnp.float32)
    up_part = jnp.dot(normed_two, weight_piece[:, 1, :], preferred_element_type=jnp.float32)
    act_part = (gate_part * jax.nn.sigmoid(gate_part) * up_part).astype(jnp.bfloat16)
    out_sum = jnp.einsum(
        "tf,df->td", act_part, weight_piece[:, 2, :], preferred_element_type=jnp.float32
    )
    gate_all = gate_part
    up_all = up_part
    gate_pre = gate_all
    up_pre = up_all
    activated = act_part
    weight_piece = lax.all_gather(ffn_weight, "fsdp", axis=2, tiled=True)
    row_count = weight_piece.shape[2]
    gate_part = gate_pre
    up_part = up_pre
    sig_part = jax.nn.sigmoid(gate_part)
    act_part_grad = jnp.dot(grad_in, weight_piece[:, 2, :], preferred_element_type=jnp.float32)
    gate_part_grad = (
        act_part_grad * up_part * sig_part * (1.0 + gate_part * (1.0 - sig_part))
    ).astype(jnp.bfloat16)
    up_part_grad = (act_part_grad * gate_part * sig_part).astype(jnp.bfloat16)
    sum_grad = jnp.einsum(
        "tf,df->td", gate_part_grad, weight_piece[:, 0, :], preferred_element_type=jnp.float32
    )
    sum_grad = sum_grad + jnp.einsum(
        "tf,df->td", up_part_grad, weight_piece[:, 1, :], preferred_element_type=jnp.float32
    )
    gate_all = gate_part_grad
    up_all = up_part_grad
    gate_grad = gate_all
    up_grad = up_all
    gate_grad, up_grad, activated = (
        lax.all_to_all(gate_grad, "fsdp", split_axis=1, concat_axis=0, tiled=True),
        lax.all_to_all(up_grad, "fsdp", split_axis=1, concat_axis=0, tiled=True),
        lax.all_to_all(activated, "fsdp", split_axis=1, concat_axis=0, tiled=True),
    )
    output = (residual + out_sum).astype(jnp.bfloat16)
    ffn_weight_grad = lax.psum_scatter(
        jnp.stack(
            [
                jnp.einsum("tc,tf->cf", rows_in, gate_grad, preferred_element_type=jnp.float32),
                jnp.einsum("tc,tf->cf", rows_in, up_grad, preferred_element_type=jnp.float32),
                jnp.einsum("tc,tf->cf", rows_out, activated, preferred_element_type=jnp.float32),
            ],
            axis=1,
        ).astype(jnp.bfloat16),
        "ctx",
        scatter_dimension=0,
        tiled=True,
    ).astype(jnp.float32)
    unit_two = residual * scale_two
    ffn_gain_term = jnp.sum(sum_grad * unit_two, axis=0)
    scaled_two = ffn_gain * sum_grad
    residual_grad = grad_in.astype(jnp.float32) + scale_two * (
        scaled_two - unit_two * jnp.mean(scaled_two * unit_two, axis=-1, keepdims=True)
    )
    residual_bf = residual_grad.astype(jnp.bfloat16)
    attn_grad = jnp.dot(residual_bf, out_full, preferred_element_type=jnp.float32).astype(
        jnp.bfloat16
    )
    out_term = jnp.einsum("td,tc->dc", residual_bf, attn_rows, preferred_element_type=jnp.float32)
    attn_grad_heads = attn_grad.reshape(local_rows, KV, groups, HD)
    row_delta = jnp.sum(attn_grad_heads.astype(jnp.float32) * attended, axis=-1).transpose(1, 2, 0)

    def backward_step(carry_state, key_pair, first_row):
        query_grad, key_grad, value_grad = carry_state
        key_part, value_part = key_pair
        row_count = key_part.shape[0]
        key_heads = key_part.reshape(row_count, KV, HD)
        value_heads = value_part.reshape(row_count, KV, HD)
        scores, allowed = masked_scores(key_heads, first_row, row_count)
        probs = jnp.where(allowed, jnp.exp(scores - log_total[..., None]), 0.0)
        value_piece = jnp.einsum(
            "kgts,tkgd->skd",
            probs.astype(jnp.bfloat16),
            attn_grad_heads,
            preferred_element_type=jnp.float32,
        )
        prob_grad = jnp.einsum(
            "tkgd,skd->kgts", attn_grad_heads, value_heads, preferred_element_type=jnp.float32
        )
        score_grad = (probs * (prob_grad - row_delta[..., None]) * score_scale).astype(jnp.bfloat16)
        query_grad = query_grad + jnp.einsum(
            "kgts,skd->tkgd", score_grad, key_heads, preferred_element_type=jnp.float32
        )
        key_piece = jnp.einsum(
            "kgts,tkgd->skd", score_grad, queries, preferred_element_type=jnp.float32
        )
        key_grad = lax.dynamic_update_slice_in_dim(
            key_grad, key_piece.reshape(row_count, KV * HD), first_row, 0
        )
        value_grad = lax.dynamic_update_slice_in_dim(
            value_grad, value_piece.reshape(row_count, KV * HD), first_row, 0
        )
        return (query_grad, key_grad, value_grad)

    start_grads = (
        jnp.zeros((local_rows, KV, groups, HD), jnp.float32),
        jnp.zeros((seq_rows, KV * HD), jnp.float32),
        jnp.zeros((seq_rows, KV * HD), jnp.float32),
    )
    grad_state = sweep_keys(
        backward_step,
        start_grads,
        (
            lax.all_gather(key_local, "ctx", axis=0, tiled=True),
            lax.all_gather(value_local, "ctx", axis=0, tiled=True),
        ),
    )
    query_grad, key_grad_all, value_grad_all = grad_state
    key_grad_own, value_grad_own = (
        lax.psum_scatter(
            key_grad_all.astype(jnp.bfloat16), "ctx", scatter_dimension=0, tiled=True
        ).astype(jnp.float32),
        lax.psum_scatter(
            value_grad_all.astype(jnp.bfloat16), "ctx", scatter_dimension=0, tiled=True
        ).astype(jnp.float32),
    )
    projected_grad = jnp.concatenate(
        [
            rotate(query_grad.reshape(local_rows, H, HD), -token_places).reshape(
                local_rows, H * HD
            ),
            rotate(key_grad_own.reshape(local_rows, KV, HD), -token_places).reshape(
                local_rows, KV * HD
            ),
            value_grad_own,
        ],
        axis=1,
    ).astype(jnp.bfloat16)
    normed_one_grad = jnp.einsum(
        "tc,dc->td", projected_grad, qkv_full, preferred_element_type=jnp.float32
    )
    qkv_term = jnp.einsum(
        "td,tc->dc", normed_one, projected_grad, preferred_element_type=jnp.float32
    )
    unit_one = inputs * scale_one
    attn_gain_term = jnp.sum(normed_one_grad * unit_one, axis=0)
    scaled_one = attn_gain * normed_one_grad
    input_grad = residual_grad + scale_one * (
        scaled_one - unit_one * jnp.mean(scaled_one * unit_one, axis=-1, keepdims=True)
    )
    qkv_grad, out_weight_grad, attn_gain_grad, ffn_gain_grad = (
        lax.psum_scatter(qkv_term, ("ctx", "fsdp"), scatter_dimension=0, tiled=True),
        lax.psum_scatter(out_term, ("ctx", "fsdp"), scatter_dimension=0, tiled=True),
        lax.psum_scatter(attn_gain_term, ("ctx", "fsdp"), scatter_dimension=0, tiled=True),
        lax.psum_scatter(ffn_gain_term, ("ctx", "fsdp"), scatter_dimension=0, tiled=True),
    )
    return (
        output[None],
        input_grad[None],
        qkv_grad,
        out_weight_grad,
        ffn_weight_grad,
        attn_gain_grad,
        ffn_gain_grad,
    )


def solution(mesh):
    return jax.shard_map(
        body,
        mesh=mesh,
        in_specs=(
            P("fsdp", "ctx", None),
            P("fsdp", "ctx", None),
            P("fsdp", "ctx"),
            P(),
            P(),
            P(),
            P("fsdp", None),
            P("fsdp", None),
            P(None, None, "fsdp"),
        ),
        out_specs=(
            P("fsdp", "ctx", None),
            P("fsdp", "ctx", None),
            P(("ctx", "fsdp"), None),
            P(("ctx", "fsdp"), None),
            P("ctx", None, "fsdp"),
            P(("ctx", "fsdp")),
            P(("ctx", "fsdp")),
        ),
        check_vma=False,
    )
```

profile of v0, /device:TPU:0, one launch (start us, length us, event | category | flops | bytes accessed | tf_op | source)
XLA Modules:
  0.0 3142.8 jit_solution(4543832504179743126)
XLA Ops:
  10.9 219.6 %all-gather.9.cloned.1.call-done = bf16[2048,3072]{1,0:T(8,128)(2,1)} async-done(((bf16[512,3072]{1,0:T(8,128)(2,1)}), bf16[2048,3072]{1,0:T(8,128)(2,1)}) %all-gather.9.cloned.1.call-update) | async-done | bytes 12582928 | tf_op jit(solution)/shard_map/all_gather | solution.py:82
  230.5 6.7 fusion.70
  241.2 18.8 all-gather.11.cloned.1.call-done
  261.5 24.4 all-gather.13.cloned.1.call-done
  287.4 33.5 %while.40 = (s32[]{:T(128)}, f32[8,4,128]{2,1,0:T(4,128)S(1)}, f32[8,4,128]{2,1,0:T(4,128)S(1)}, f32[8,4,128,64]{2,3,1,0:T(8,128)}, s32[16]{0:T(128)S(1)}, /*ind...) while((s32[]{:T(128)}, f32[8,4,128]{2,1,0:T(4,128)S(1)}, ...), condition=%wide.region_6.7_spmd.clone, body=%wide.region_2.6_spmd.clone.sunk | while | flops 565045760 | bytes 65024804 | solution.py:53
  288.6 4.6 fusion.135
  293.1 5.8 fusion.136
  300.8 4.1 fusion.138
  306.0 4.6 fusion.135
  310.6 4.7 fusion.136
  316.5 4.4 fusion.138
  320.9 2.5 bitcast_convert_fusion
  323.4 113.5 %all-gather.15.cloned.1.call-done = bf16[2048,2048]{1,0:T(8,128)(2,1)} async-done(((bf16[512,2048]{1,0:T(8,128)(2,1)}), bf16[2048,2048]{1,0:T(8,128)(2,1)}) %all-gather.15.cloned.1.call-update) | async-done | bytes 8388624 | tf_op jit(solution)/shard_map/all_gather | solution.py:83
  436.9 6.5 multiply_reduce_fusion.2
  446.2 1650.2 %all-gather.17.cloned.1.call-done = bf16[2048,3,8192]{2,0,1:T(8,128)(2,1)} async-done(((bf16[2048,3,2048]{2,0,1:T(8,128)(2,1)}), bf16[2048,3,8192]{2,0,1:T(8,128)(2,1)}) %all-gather.17.cloned.1.call-update) | async-done | bytes 100663312 | tf_op jit(solution)/shard_map/all_gather | solution.py:152
  2096.4 15.5 fusion.36
  2112.0 15.2 fusion.38
  2127.1 17.6 multiply_convert_fusion
  2147.6 4.7 all-to-all-start.1
  2152.3 17.3 fusion.35
  2169.7 20.1 multiply_reduce_fusion
  2192.6 5.5 convolution_convert_fusion
  2199.5 3.2 copy.109
  2204.1 29.0 all-to-all-done.1
  2233.1 4.5 all-to-all-start
  2240.0 40.3 %while.41 = (s32[]{:T(128)}, f32[128,8,4,64]{0,3,2,1:T(8,128)S(1)}, bf16[1024,512]{0,1:T(8,128)(2,1)}, bf16[1024,512]{0,1:T(8,128)(2,1)}, bf16[1024,512]{0,1:T(8...) while((s32[]{:T(128)}, f32[128,8,4,64]{0,3,2,1:T(8,128)S(1)}, ...), condition=%wide.region_12.13_spmd.clone, body=%wide.region_10.12_spmd.clone.sunk | while | flops 1370069504 | bytes 124515376 | solution.py:53
  2242.5 6.0 fusion.151
  2248.5 3.1 fusion.152
  2251.7 5.6 fusion.153
  2262.7 6.0 fusion.151
  2268.7 3.1 fusion.152
  2271.9 5.6 fusion.153
  2282.7 3.2 copy.107
  2286.2 4.7 all-to-all-start.2
  2292.8 10.4 convert_bitcast_fusion.1
  2303.2 8.5 convert_bitcast_fusion.2
  2311.7 27.3 all-to-all-done.2
  2339.1 10.1 convert_bitcast_fusion
  2349.2 14.2 pad_maximum_fusion
  2364.7 11.5 fusion.66
  2379.9 16.4 fusion.63
  2397.6 17.3 fusion.44
  2414.9 9.4 fusion.56
  2424.3 39.6 %all-reduce.2 = (f32[2048]{0:T(1024)S(1)}, f32[2048]{0:T(1024)S(1)}) all-reduce(f32[2048]{0:T(1024)S(1)} %get-tuple-element.684, f32[2048]{0:T(1024)S(1)} %copy-done.33), channel_id=8, replica_groups=mesh['ctx'=8,'fsdp'=4] {'ctx','fsdp'}, use_global_device_ids=true, to_apply=%region_20.21.clone | all-reduce | flops 4096 | bytes 32768
  2466.4 54.5 %reduce-scatter.14.cloned.1.call-done = bf16[256,3,2048]{2,0,1:T(8,128)(2,1)} async-done(((bf16[2048,3,2048]{2,0,1:T(8,128)(2,1)}), bf16[256,3,2048]{2,0,1:T(8,128)(2,1)}) %reduce-scatter.14.cloned.1.call-update) | async-done | bytes 3145744 | tf_op jit(solution)/shard_map/reduce_scatter | solution.py:190
  2520.9 5.4 convert_element_type.141
  2526.3 358.1 %reduce-scatter.12.cloned.1.call-done = f32[64,2048]{1,0:T(8,128)} async-done(((f32[2048,2048]{1,0:T(8,128)}), f32[64,2048]{1,0:T(8,128)}) %reduce-scatter.12.cloned.1.call-update) | async-done | bytes 524304 | tf_op jit(solution)/shard_map/reduce_scatter | solution.py:297
  2884.4 251.3 %reduce-scatter.10.cloned.1.call-done = f32[64,3072]{1,0:T(8,128)} async-done(((f32[2048,3072]{1,0:T(8,128)}), f32[64,3072]{1,0:T(8,128)}) %reduce-scatter.10.cloned.1.call-update) | async-done | bytes 786448 | tf_op jit(solution)/shard_map/reduce_scatter | solution.py:296
  (209 shorter events, 53.3 us)
Async XLA Ops:
  7.2 223.3 %all-gather.9.cloned.1.call-start = ((), (), s32[]{:S(2)}) async-start(), calls=%async_computation.8 | async-start | bytes 15728640 | tf_op jit(solution)/shard_map/all_gather | solution.py:82
  7.9 252.1 %all-gather.11.cloned.1.call-start = ((), (), s32[]{:S(2)}) async-start(), calls=%async_computation.9 | async-start | bytes 1179648 | tf_op jit(solution)/shard_map/all_gather | solution.py:135
  10.9 226.3 %copy-start.31 = (f32[128]{0:T(128)}, f32[128]{0:T(128)S(1)}, u32[]{:S(2)}) copy-start(f32[128]{0:T(128)S(1)} %add_rsqrt_fusion.1) | copy-start | bytes 1540
  238.3 47.6 %all-gather.13.cloned.1.call-start = ((), (), s32[]{:S(2)}) async-start(), calls=%async_computation.10 | async-start | bytes 1179648 | tf_op jit(solution)/shard_map/all_gather | solution.py:136
  239.0 197.9 %all-gather.15.cloned.1.call-start = ((), (), s32[]{:S(2)}) async-start(), calls=%async_computation.11 | async-start | bytes 10485760 | tf_op jit(solution)/shard_map/all_gather | solution.py:83
  239.6 1856.8 %all-gather.17.cloned.1.call-start = ((), (), s32[]{:S(2)}) async-start(), calls=%async_computation.12 | async-start | bytes 125829120 | tf_op jit(solution)/shard_map/all_gather | solution.py:152
  240.2 2052.6 %all-gather.19.cloned.1.call-start = ((), (), s32[]{:S(2)}) async-start(), calls=%async_computation.15 | async-start | bytes 2621440 | tf_op jit(solution)/shard_map/all_gather | solution.py:149
  287.4 149.6 %copy-start.7 = (bf16[1,128,2048]{2,1,0:T(8,128)(2,1)S(1)}, bf16[1,128,2048]{2,1,0:T(8,128)(2,1)}, u32[]{:S(2)}) copy-start(bf16[1,128,2048]{2,1,0:T(8,128)(2,1)} %param.13) | copy-start | bytes 1572868
  293.1 7.6 copy-start
  310.6 5.9 copy-start
  320.9 125.3 %copy-start.3 = (bf16[1024,512]{0,1:T(8,128)(2,1)}, bf16[1024,512]{0,1:T(8,128)(2,1)S(1)}, u32[]{:S(2)}) copy-start(bf16[1024,512]{0,1:T(8,128)(2,1)S(1)} %get-tuple-element.1013) | copy-start | bytes 3145732
  320.9 123.6 %copy-start.30 = (f32[2048]{0:T(1024)S(1)}, f32[2048]{0:T(1024)}, u32[]{:S(2)}) copy-start(f32[2048]{0:T(1024)} %param.18) | copy-start | bytes 24580
  445.4 1866.3 %all-gather.21.cloned.1.call-start = ((), (), s32[]{:S(2)}) async-start(), calls=%async_computation.17 | async-start | bytes 2621440 | tf_op jit(solution)/shard_map/all_gather | solution.py:150
  446.2 1665.7 %copy-start.24 = (bf16[128,2048]{1,0:T(8,128)(2,1)S(1)}, bf16[128,2048]{1,0:T(8,128)(2,1)}, u32[]{:S(2)}) copy-start(bf16[128,2048]{1,0:T(8,128)(2,1)} %multiply_convert_fusion.3) | copy-start | bytes 1572868
  2144.7 1.3 copy-start.23
  2147.6 85.5 %all-to-all-start.1 = ((bf16[128,4,2048]{2,0,1:T(8,128)(2,1)}), bf16[128,4,2048]{2,0,1:T(8,128)(2,1)}, u32[]{:S(2)}, u32[]{:S(2)}) async-start(bf16[128,4,2048]{2,0,1:T(8,128)(2,1)} %bitcast.282), calls=%async_computation.3 | async-start | bytes 4194304 | tf_op jit(solution)/shard_map/all_to_all | solution.py:186
  2169.7 20.1 copy-start.25
  2233.1 53.1 %all-to-all-start = ((bf16[128,4,2048]{2,0,1:T(8,128)(2,1)}), bf16[128,4,2048]{2,0,1:T(8,128)(2,1)}, u32[]{:S(2)}, u32[]{:S(2)}) async-start(bf16[128,4,2048]{2,0,1:T(8,128)(2,1)} %bitcast.280), calls=%async_computation.2 | async-start | bytes 4194304 | tf_op jit(solution)/shard_map/all_to_all | solution.py:185
  2237.5 139.9 %reduce-scatter.16.cloned.1.call-start = ((), (), s32[]{:S(2)}) async-start(), calls=%async_computation.18 | async-start | bytes 1179648
  2240.8 1.6 copy-start.4
  2242.2 6.3 copy-start.2
  2251.7 5.6 copy-start.1
  2251.7 7.0 copy-start.14
  2251.7 7.0 copy-start.16
  2251.7 8.5 copy-start.22
  2258.9 1.3 copy-start.17
  2261.0 1.6 copy-start.4
  2262.3 6.3 copy-start.2
  2271.8 5.6 copy-start.1
  2271.8 7.0 copy-start.14
  2271.8 7.0 copy-start.16
  2271.9 8.5 copy-start.22
  2280.4 10.6 copy-start.18
  2286.2 52.9 %all-to-all-start.2 = ((bf16[128,4,2048]{2,0,1:T(8,128)(2,1)}), bf16[128,4,2048]{2,0,1:T(8,128)(2,1)}, u32[]{:S(2)}, u32[]{:S(2)}) async-start(bf16[128,4,2048]{2,0,1:T(8,128)(2,1)} %bitcast.281), calls=%async_computation.4 | async-start | bytes 4194304 | tf_op jit(solution)/shard_map/all_to_all | solution.py:187
  2290.9 87.9 %reduce-scatter.18.cloned.1.call-start = ((), (), s32[]{:S(2)}) async-start(), calls=%async_computation.19 | async-start | bytes 1179648
  2292.3 228.6 %reduce-scatter.14.cloned.1.call-start = ((), (), s32[]{:S(2)}) async-start(), calls=%async_computation.16 | async-start | bytes 28311552 | tf_op jit(solution)/shard_map/reduce_scatter | solution.py:190
  2292.8 10.4 copy-start.34
  2339.1 10.2 copy-start.11
  2339.1 10.2 copy-start.12
  2363.4 1.4 copy-start.13
  2363.4 521.0 %reduce-scatter.12.cloned.1.call-start = ((), (), s32[]{:S(2)}) async-start(), calls=%async_computation.14 | async-start | bytes 17301504 | tf_op jit(solution)/shard_map/reduce_scatter | solution.py:297
  2376.3 3.6 copy-start.8
  2376.3 3.6 copy-start.26
  2376.3 3.6 copy-start.32
  2376.3 759.4 %reduce-scatter.10.cloned.1.call-start = ((), (), s32[]{:S(2)}) async-start(), calls=%async_computation.13 | async-start | bytes 25952256 | tf_op jit(solution)/shard_map/reduce_scatter | solution.py:296
  2377.4 18.9 copy-start.19
  2397.6 17.3 copy-start.20
  2414.9 9.4 copy-start.33
  (12 other events, 11.6 us)
Sparse Core Ops, SparseCore 0:
  9.5 220.9 all-gather.8
  238.4 21.5 all-gather.10
  262.5 23.3 all-gather.12
  287.3 149.5 all-gather.14
  438.4 1658.0 all-gather.16
  2098.4 43.8 all-gather.18
  2143.9 83.2 all-gather.20
  2282.9 37.2 reduce-scatter.15
  2323.9 35.9 reduce-scatter.17
  2363.5 157.3 reduce-scatter.13
  2523.8 360.6 reduce-scatter.11
  2891.3 244.3 reduce-scatter.9
where the time goes:
time: 3150 us; the launch traced here: 3140 us
  waiting for transfers between devices  2750 us (87%)
  matrix products  241 us (8%)
  other arithmetic  43.7 us (1%)
  blocking collectives  39.6 us (1%)
  local copies, waits for them, and re-layouts  38.9 us (1%)
    all_gather x1, waiting for transfers between devices, body(): weight_piece = lax.all_gather(ffn_weight, 'fsdp', axis=2, tiled=True)  1650 us
    reduce_scatter x1, waiting for transfers between devices, body(): lax.psum_scatter(out_term, ('ctx', 'fsdp'), scatter_dimension=0, tiled=True)  358 us
    reduce_scatter x1, waiting for transfers between devices, body(): lax.psum_scatter(qkv_term, ('ctx', 'fsdp'), scatter_dimension=0, tiled=True)  251 us
    all_gather x1, waiting for transfers between devices, body(): lax.all_gather(qkv_weight, 'fsdp', axis=0, tiled=True)  220 us
    all_gather x1, waiting for transfers between devices, body(): lax.all_gather(out_weight, 'fsdp', axis=0, tiled=True)  114 us
  transfers between devices with their start and end apart: 15, of which 11 were waited for; matrix products, arithmetic and copies ran while one was open for 10% of the time, Pallas kernels for 0%

commit v1 on v0

--- a/solution.py
+++ b/solution.py
@@ -79,7 +79,9 @@
     scale_one = norm_scale(inputs)
     normed_one = (inputs * scale_one * attn_gain).astype(jnp.bfloat16)
     qkv_full, out_full = (
-        lax.all_gather(qkv_weight, "fsdp", axis=0, tiled=True),
+        jnp.concatenate(
+            lax.all_to_all(jnp.stack([qkv_weight] * lax.axis_size("fsdp")), "fsdp", 0, 0), axis=0
+        ),
         lax.all_gather(out_weight, "fsdp", axis=0, tiled=True),
     )
     projected = jnp.dot(normed_one, qkv_full, preferred_element_type=jnp.float32)

time: 3150 us -> 3210 us (1.019)
  waiting for transfers between devices: 2750 us -> 2800 us
    all_to_all x0 -> x1, waiting for transfers between devices: none -> 273 us  [body(): lax.all_to_all(jnp.stack([qkv_weight] * lax.axis_size('fsdp')), 'fsdp', 0...]
    all_gather x1 -> x0, waiting for transfers between devices: 220 us -> none  [body(): lax.all_gather(qkv_weight, 'fsdp', axis=0, tiled=True)]
  transfers between devices with their start and end apart: 15 -> 15, of which waited for: 11 -> 11; matrix products, arithmetic and copies ran while one was open for 10% -> 9% of each run, Pallas kernels for 0% -> 0%
where the time goes in v1:
time: 3210 us
  waiting for transfers between devices  2800 us (87%)
  matrix products  239 us (7%)
  local copies, waits for them, and re-layouts  44.7 us (1%)
  other arithmetic  42 us (1%)
  blocking collectives  40 us (1%)
    all_gather x1, waiting for transfers between devices, body(): weight_piece = lax.all_gather(ffn_weight, 'fsdp', axis=2, tiled=True)  1650 us
    reduce_scatter x1, waiting for transfers between devices, body(): lax.psum_scatter(out_term, ('ctx', 'fsdp'), scatter_dimension=0, tiled=True)  358 us
    all_to_all x1, waiting for transfers between devices, body(): lax.all_to_all(jnp.stack([qkv_weight] * lax.axis_size('fsdp')), 'fsdp', 0...  273 us
    reduce_scatter x1, waiting for transfers between devices, body(): lax.psum_scatter(qkv_term, ('ctx', 'fsdp'), scatter_dimension=0, tiled=True)  251 us
    all_gather x1, waiting for transfers between devices, body(): lax.all_gather(out_weight, 'fsdp', axis=0, tiled=True)  114 us
  transfers between devices with their start and end apart: 15, of which 11 were waited for; matrix products, arithmetic and copies ran while one was open for 9% of the time, Pallas kernels for 0%

profile of v1, /device:TPU:0, one launch (start us, length us, event | category | flops | bytes accessed | tf_op | source)
XLA Modules:
  0.0 3207.7 jit_solution(2866039640158242930)
XLA Ops:
  7.2 8.0 stack.23
  15.2 6.5 all-to-all-start
  22.9 273.4 %all-to-all-done = bf16[4,512,3072]{2,1,0:T(8,128)(2,1)} async-done(((bf16[4,512,3072]{2,1,0:T(8,128)(2,1)}), bf16[4,512,3072]{2,1,0:T(8,128)(2,1)}, u32[]{:S(2)}, u32[]{:S(2)}) %all-to-all-start) | async-done | bytes 12582944 | tf_op jit(solution)/shard_map/all_to_all | solution.py:83
  296.3 6.5 fusion.67
  307.2 19.4 all-gather.8.cloned.1.call-done
  328.1 24.4 all-gather.10.cloned.1.call-done
  354.0 33.5 %while.40 = (s32[]{:T(128)}, f32[8,4,128]{2,1,0:T(4,128)S(1)}, f32[8,4,128]{2,1,0:T(4,128)S(1)}, f32[8,4,128,64]{2,3,1,0:T(8,128)}, s32[16]{0:T(128)S(1)}, /*ind...) while((s32[]{:T(128)}, f32[8,4,128]{2,1,0:T(4,128)S(1)}, ...), condition=%wide.region_6.7_spmd.clone, body=%wide.region_2.6_spmd.clone.sunk | while | flops 565045760 | bytes 65024804 | solution.py:53
  355.1 4.5 fusion.144
  359.7 5.8 fusion.145
  367.3 4.1 fusion.147
  372.6 4.5 fusion.144
  377.1 4.7 fusion.145
  383.0 4.4 fusion.147
  390.0 113.7 %all-gather.12.cloned.1.call-done = bf16[2048,2048]{1,0:T(8,128)(2,1)} async-done(((bf16[512,2048]{1,0:T(8,128)(2,1)}), bf16[2048,2048]{1,0:T(8,128)(2,1)}) %all-gather.12.cloned.1.call-update) | async-done | bytes 8388624 | tf_op jit(solution)/shard_map/all_gather | solution.py:85
  503.7 6.5 multiply_reduce_fusion.2
  512.8 1650.4 %all-gather.14.cloned.1.call-done = bf16[2048,3,8192]{2,0,1:T(8,128)(2,1)} async-done(((bf16[2048,3,2048]{2,0,1:T(8,128)(2,1)}), bf16[2048,3,8192]{2,0,1:T(8,128)(2,1)}) %all-gather.14.cloned.1.call-update) | async-done | bytes 100663312 | tf_op jit(solution)/shard_map/all_gather | solution.py:154
  2163.2 15.5 fusion.36
  2178.7 15.1 fusion.38
  2193.8 17.6 multiply_convert_fusion
  2214.3 4.7 all-to-all-start.2
  2219.0 17.3 fusion.35
  2236.4 20.1 multiply_reduce_fusion
  2259.3 4.7 convolution_convert_fusion
  2265.0 3.2 copy.109
  2269.8 29.9 all-to-all-done.2
  2299.7 4.5 all-to-all-start.1
  2306.8 38.7 %while.41 = (s32[]{:T(128)}, f32[128,8,4,64]{0,3,2,1:T(8,128)S(1)}, bf16[1024,512]{0,1:T(8,128)(2,1)}, bf16[1024,512]{0,1:T(8,128)(2,1)}, bf16[1024,512]{0,1:T(8...) while((s32[]{:T(128)}, f32[128,8,4,64]{0,3,2,1:T(8,128)S(1)}, ...), condition=%wide.region_12.13_spmd.clone, body=%wide.region_10.12_spmd.clone.sunk | while | flops 1370069504 | bytes 120321008 | solution.py:53
  2308.5 6.0 fusion.160
  2314.5 3.1 fusion.161
  2317.7 5.6 fusion.162
  2327.8 6.0 fusion.160
  2337.0 5.6 fusion.162
  2347.9 3.2 copy.107
  2352.8 4.4 all-to-all-start.3
  2358.9 10.4 convert_bitcast_fusion.1
  2369.3 8.4 convert_bitcast_fusion.2
  2377.6 27.4 all-to-all-done.3
  2405.0 10.1 convert_bitcast_fusion
  2415.2 14.2 pad_maximum_fusion
  2430.7 12.1 fusion.78
  2446.3 16.0 fusion.69
  2463.6 17.3 fusion.44
  2480.9 9.4 fusion.58
  2490.3 40.0 %all-reduce.2 = (f32[2048]{0:T(1024)S(1)}, f32[2048]{0:T(1024)S(1)}) all-reduce(f32[2048]{0:T(1024)S(1)} %get-tuple-element.684, f32[2048]{0:T(1024)S(1)} %copy-done.30), channel_id=8, replica_groups=mesh['ctx'=8,'fsdp'=4] {'ctx','fsdp'}, use_global_device_ids=true, to_apply=%region_20.21.clone | all-reduce | flops 4096 | bytes 32768
  2532.7 53.4 %reduce-scatter.14.cloned.1.call-done = bf16[256,3,2048]{2,0,1:T(8,128)(2,1)} async-done(((bf16[2048,3,2048]{2,0,1:T(8,128)(2,1)}), bf16[256,3,2048]{2,0,1:T(8,128)(2,1)}) %reduce-scatter.14.cloned.1.call-update) | async-done | bytes 3145744 | tf_op jit(solution)/shard_map/reduce_scatter | solution.py:192
  2586.2 5.4 convert_element_type.152
  2591.6 357.9 %reduce-scatter.12.cloned.1.call-done = f32[64,2048]{1,0:T(8,128)} async-done(((f32[2048,2048]{1,0:T(8,128)}), f32[64,2048]{1,0:T(8,128)}) %reduce-scatter.12.cloned.1.call-update) | async-done | bytes 524304 | tf_op jit(solution)/shard_map/reduce_scatter | solution.py:299
  2949.5 251.4 %reduce-scatter.10.cloned.1.call-done = f32[64,3072]{1,0:T(8,128)} async-done(((f32[2048,3072]{1,0:T(8,128)}), f32[64,3072]{1,0:T(8,128)}) %reduce-scatter.10.cloned.1.call-update) | async-done | bytes 786448 | tf_op jit(solution)/shard_map/reduce_scatter | solution.py:298
  (201 shorter events, 56.0 us)
Async XLA Ops:
  15.2 6.6 copy-start.32
  15.2 7.5 copy-start.7
  15.2 281.2 %copy-start.22 = (f32[2048]{0:T(1024)S(1)}, f32[2048]{0:T(1024)}, u32[]{:S(2)}) copy-start(f32[2048]{0:T(1024)} %param.17) | copy-start | bytes 24580
  15.2 281.2 %all-to-all-start = ((bf16[4,512,3072]{2,1,0:T(8,128)(2,1)}), bf16[4,512,3072]{2,1,0:T(8,128)(2,1)}, u32[]{:S(2)}, u32[]{:S(2)}) async-start(bf16[4,512,3072]{2,1,0:T(8,128)(2,1)} %stack.23), calls=%async_computation | async-start | bytes 25165824 | tf_op jit(solution)/shard_map/all_to_all | solution.py:83
  21.7 304.9 %all-gather.8.cloned.1.call-start = ((), (), s32[]{:S(2)}) async-start(), calls=%async_computation.9 | async-start | bytes 1179648 | tf_op jit(solution)/shard_map/all_gather | solution.py:137
  22.9 279.9 %copy-start.28 = (f32[128]{0:T(128)}, f32[128]{0:T(128)S(1)}, u32[]{:S(2)}) copy-start(f32[128]{0:T(128)S(1)} %add_rsqrt_fusion.1) | copy-start | bytes 1540
  303.9 48.5 %all-gather.10.cloned.1.call-start = ((), (), s32[]{:S(2)}) async-start(), calls=%async_computation.10 | async-start | bytes 1179648 | tf_op jit(solution)/shard_map/all_gather | solution.py:138
  304.7 199.0 %all-gather.12.cloned.1.call-start = ((), (), s32[]{:S(2)}) async-start(), calls=%async_computation.11 | async-start | bytes 10485760 | tf_op jit(solution)/shard_map/all_gather | solution.py:85
  305.4 1857.7 %all-gather.14.cloned.1.call-start = ((), (), s32[]{:S(2)}) async-start(), calls=%async_computation.12 | async-start | bytes 125829120 | tf_op jit(solution)/shard_map/all_gather | solution.py:154
  306.0 2052.8 %all-gather.16.cloned.1.call-start = ((), (), s32[]{:S(2)}) async-start(), calls=%async_computation.15 | async-start | bytes 2621440 | tf_op jit(solution)/shard_map/all_gather | solution.py:151
  359.7 7.7 copy-start
  377.1 5.9 copy-start
  387.4 125.3 %copy-start.3 = (bf16[1024,512]{0,1:T(8,128)(2,1)}, bf16[1024,512]{0,1:T(8,128)(2,1)S(1)}, u32[]{:S(2)}) copy-start(bf16[1024,512]{0,1:T(8,128)(2,1)S(1)} %get-tuple-element.1014) | copy-start | bytes 3145732
  387.4 123.8 %copy-start.27 = (f32[2048]{0:T(1024)S(1)}, f32[2048]{0:T(1024)}, u32[]{:S(2)}) copy-start(f32[2048]{0:T(1024)} %param.18) | copy-start | bytes 24580
  512.2 1865.5 %all-gather.18.cloned.1.call-start = ((), (), s32[]{:S(2)}) async-start(), calls=%async_computation.17 | async-start | bytes 2621440 | tf_op jit(solution)/shard_map/all_gather | solution.py:152
  512.8 1665.9 %copy-start.20 = (bf16[128,2048]{1,0:T(8,128)(2,1)S(1)}, bf16[128,2048]{1,0:T(8,128)(2,1)}, u32[]{:S(2)}) copy-start(bf16[128,2048]{1,0:T(8,128)(2,1)} %multiply_convert_fusion.3) | copy-start | bytes 1572868
  2211.4 1.3 copy-start.19
  2214.3 85.4 %all-to-all-start.2 = ((bf16[128,4,2048]{2,0,1:T(8,128)(2,1)}), bf16[128,4,2048]{2,0,1:T(8,128)(2,1)}, u32[]{:S(2)}, u32[]{:S(2)}) async-start(bf16[128,4,2048]{2,0,1:T(8,128)(2,1)} %bitcast.309), calls=%async_computation.4 | async-start | bytes 4194304 | tf_op jit(solution)/shard_map/all_to_all | solution.py:188
  2236.4 20.1 copy-start.21
  2299.7 53.1 %all-to-all-start.1 = ((bf16[128,4,2048]{2,0,1:T(8,128)(2,1)}), bf16[128,4,2048]{2,0,1:T(8,128)(2,1)}, u32[]{:S(2)}, u32[]{:S(2)}) async-start(bf16[128,4,2048]{2,0,1:T(8,128)(2,1)} %bitcast.307), calls=%async_computation.3 | async-start | bytes 4194304 | tf_op jit(solution)/shard_map/all_to_all | solution.py:187
  2304.1 139.8 %reduce-scatter.16.cloned.1.call-start = ((), (), s32[]{:S(2)}) async-start(), calls=%async_computation.18 | async-start | bytes 1179648
  2306.8 1.6 copy-start.4
  2308.2 6.3 copy-start.2
  2317.7 5.6 copy-start.1
  2317.7 7.0 copy-start.14
  2317.7 7.0 copy-start.16
  2324.9 1.3 copy-start.17
  2326.2 1.6 copy-start.4
  2327.5 6.3 copy-start.2
  2337.0 5.6 copy-start.1
  2337.0 7.0 copy-start.14
  2337.0 7.0 copy-start.16
  2344.2 1.3 copy-start.17
  2345.5 11.8 copy-start.18
  2352.8 52.3 %all-to-all-start.3 = ((bf16[128,4,2048]{2,0,1:T(8,128)(2,1)}), bf16[128,4,2048]{2,0,1:T(8,128)(2,1)}, u32[]{:S(2)}, u32[]{:S(2)}) async-start(bf16[128,4,2048]{2,0,1:T(8,128)(2,1)} %bitcast.308), calls=%async_computation.5 | async-start | bytes 4194304 | tf_op jit(solution)/shard_map/all_to_all | solution.py:189
  2357.2 88.0 %reduce-scatter.18.cloned.1.call-start = ((), (), s32[]{:S(2)}) async-start(), calls=%async_computation.19 | async-start | bytes 1179648
  2358.6 227.6 %reduce-scatter.14.cloned.1.call-start = ((), (), s32[]{:S(2)}) async-start(), calls=%async_computation.16 | async-start | bytes 28311552 | tf_op jit(solution)/shard_map/reduce_scatter | solution.py:192
  2358.9 10.4 copy-start.31
  2405.0 10.1 copy-start.11
  2405.0 10.1 copy-start.12
  2429.3 1.4 copy-start.13
  2429.4 520.2 %reduce-scatter.12.cloned.1.call-start = ((), (), s32[]{:S(2)}) async-start(), calls=%async_computation.14 | async-start | bytes 17301504 | tf_op jit(solution)/shard_map/reduce_scatter | solution.py:299
  2442.8 3.4 copy-start.8
  2442.8 3.4 copy-start.23
  2442.8 3.4 copy-start.29
  2442.8 758.1 %reduce-scatter.10.cloned.1.call-start = ((), (), s32[]{:S(2)}) async-start(), calls=%async_computation.13 | async-start | bytes 25952256 | tf_op jit(solution)/shard_map/reduce_scatter | solution.py:298
  2462.3 1.3 copy-start.10
  2480.9 9.4 copy-start.30
  (8 other events, 7.5 us)
Sparse Core Ops, SparseCore 0:
  304.1 22.4 all-gather.7
  329.1 23.3 all-gather.9
  354.0 149.5 all-gather.11
  505.1 1658.0 all-gather.13
  2165.2 43.8 all-gather.15
  2210.5 83.1 all-gather.17
  2348.0 37.2 reduce-scatter.15
  2389.1 35.9 reduce-scatter.17
  2429.5 156.6 reduce-scatter.13
  2588.9 360.5 reduce-scatter.11
  2956.5 244.3 reduce-scatter.9
